TPU v7x, 32 devices: a whole 2x2x4 slice. The times are simulated.
32 devices in a mesh: dp: 16 (over z, y, core), expert: 2 (over x).
Axes of the slice: x: 2, y: 2, z: 4, core: 2. Of those that a mesh axis runs over, the one named last changes fastest.
Arguments:
- tokens: bfloat16 [4096, 2048], P(('dp', 'expert')), may hold values from -6 to 6
- cotangent: bfloat16 [4096, 2048], P(('dp', 'expert')), may hold values from -6 to 6
- expert_ids: int32 [4096, 8], P(('dp', 'expert')), may hold values from 0 to 127, as said below
- route_weights: float32 [4096, 8], P(('dp', 'expert')), may hold values from 0.1 to 1
- join_groups: int32 [16], replicated, may hold values from 0 to 1
- w_gate: bfloat16 [2048, 1024], P('dp', 'expert'), may hold values from -0.125 to 0.125
- w_up: bfloat16 [2048, 1024], P('dp', 'expert'), may hold values from -0.125 to 0.125
- w_down: bfloat16 [2048, 1024], P('dp', 'expert'), may hold values from -0.1875 to 0.1875
Outputs:
- mixed: bfloat16 [4096, 2048], P(('dp', 'expert'))
- grad_gate: bfloat16 [2048, 1024], P('dp', 'expert')
- grad_up: bfloat16 [2048, 1024], P('dp', 'expert')
- grad_down: bfloat16 [2048, 1024], P('dp', 'expert')
Inputs may be any that keep to these rules, and one draw needn't show every extreme that they name: `expert_ids`: each row names 8 different experts; the rows of one device name expert 0 at most 16 times, and the rows of some device exactly 16 times.
All inputs are finite; a program needn't handle non-finite values.
Results may differ from a plain program's by a relative error of at most 0.014.
Values may be sent and summed in bfloat16 or wider, within the bound.
A program may use at most 64 MiB of HBM per device.

v0:
```python
import jax
import jax.numpy as jnp
from jax import lax
from jax.sharding import PartitionSpec as P


def per_device(tokens, cotangent, expert_ids, route_weights, join_groups, w_gate, w_up, w_down):
    highest = lax.Precision.HIGHEST
    tok_count = tokens.shape[0]
    slot_count = tok_count // 8
    slice_width = w_gate.shape[1]
    chosen_mask = expert_ids == 0
    routed = jnp.any(chosen_mask, -1)
    weight = jnp.sum(jnp.where(chosen_mask, route_weights, 0.0), -1)
    places = jnp.cumsum(routed.astype(jnp.int32)) - 1
    slot_ids = jnp.arange(slot_count, dtype=jnp.int32)
    chooser = ((places[None, :] == slot_ids[:, None]) & routed[None, :]).astype(jnp.float32)
    chooser_half = chooser.astype(jnp.bfloat16)
    picked_local = jnp.dot(chooser_half, tokens, preferred_element_type=jnp.float32).astype(
        jnp.bfloat16
    )
    picked = lax.all_gather(picked_local, "expert", axis=0, tiled=True)
    gate_acts = jnp.dot(
        picked, lax.all_gather(w_gate, "dp", axis=0, tiled=True), preferred_element_type=jnp.float32
    )
    up_acts = jnp.dot(
        picked, lax.all_gather(w_up, "dp", axis=0, tiled=True), preferred_element_type=jnp.float32
    )
    hidden = (jax.nn.silu(gate_acts) * up_acts).astype(jnp.bfloat16)
    trans_dims = (((1,), (1,)), ((), ()))
    full_down = lax.all_gather(w_down, "dp", axis=0, tiled=True)
    partial_out = lax.dot_general(hidden, full_down, trans_dims, preferred_element_type=jnp.float32)
    out_rows = lax.psum_scatter(
        partial_out.astype(jnp.bfloat16), "expert", scatter_dimension=0, tiled=True
    ).astype(jnp.float32)
    placed = lax.dot_general(
        chooser,
        out_rows,
        (((0,), (0,)), ((), ())),
        precision=highest,
        preferred_element_type=jnp.float32,
    )
    mixed = (placed * weight[:, None]).astype(jnp.bfloat16)
    scaled = cotangent.astype(jnp.float32) * weight[:, None]
    dpicked_local = jnp.dot(
        chooser, scaled, precision=highest, preferred_element_type=jnp.float32
    ).astype(jnp.bfloat16)
    dpicked = lax.all_gather(dpicked_local, "expert", axis=0, tiled=True)
    hidden_grad = jnp.dot(dpicked, full_down, preferred_element_type=jnp.float32)
    sigma_gate = jax.nn.sigmoid(gate_acts)
    dgate = (hidden_grad * up_acts * sigma_gate * (1.0 + gate_acts * (1.0 - sigma_gate))).astype(
        jnp.bfloat16
    )
    dup = (hidden_grad * gate_acts * sigma_gate).astype(jnp.bfloat16)
    group_total = lax.axis_size("dp")
    mine = jnp.arange(group_total, dtype=jnp.int32) == lax.axis_index("dp")
    active = 1.0 - jnp.sum(jnp.where(mine, join_groups, 0)).astype(jnp.float32)
    col_dims = (((0,), (0,)), ((), ()))

    def term_of(left, right):
        return active * lax.dot_general(left, right, col_dims, preferred_element_type=jnp.float32)

    summed = lax.psum_scatter(
        jnp.concatenate(
            [term_of(picked, dgate), term_of(picked, dup), term_of(dpicked, hidden)], axis=1
        ),
        "dp",
        scatter_dimension=0,
        tiled=True,
    )
    grad_gate = summed[:, :slice_width]
    grad_up = summed[:, slice_width : 2 * slice_width]
    grad_down = summed[:, 2 * slice_width :]
    return (
        mixed,
        grad_gate.astype(jnp.bfloat16),
        grad_up.astype(jnp.bfloat16),
        grad_down.astype(jnp.bfloat16),
    )


def solution(mesh):
    in_specs = (
        P(("dp", "expert"), None),
        P(("dp", "expert"), None),
        P(("dp", "expert"), None),
        P(("dp", "expert"), None),
        P(),
        P("dp", "expert"),
        P("dp", "expert"),
        P("dp", "expert"),
    )
    out_specs = (P(("dp", "expert"), None), P("dp", "expert"), P("dp", "expert"), P("dp", "expert"))
    return jax.shard_map(
        per_device, mesh=mesh, in_specs=in_specs, out_specs=out_specs, check_vma=False
    )
```

profile of v0, /device:TPU:0, one launch (start us, length us, event | category | flops | bytes accessed | tf_op | source)
XLA Modules:
  0.0 300.2 jit_solution(16604740441010829208)
XLA Ops:
  7.2 0.0 copy-start
  7.2 0.0 all-gather.4.cloned.1.call-start
  7.2 0.7 all-gather.4.cloned.1.call-update
  7.9 0.0 all-gather.6.cloned.1.call-start
  8.0 0.7 all-gather.6.cloned.1.call-update
  8.7 0.0 all-gather.8.cloned.1.call-start
  8.7 0.7 all-gather.8.cloned.1.call-update
  9.4 0.0 reduce-scatter.3.cloned.1.call-start
  9.5 1.3 fusion.15
  11.4 0.7 select_reduce_fusion
  12.1 0.1 copy.16
  12.3 0.2 reduce-window.8
  12.4 0.1 add_reduce_fusion
  12.5 1.6 convolution_convert_fusion.1
  14.2 5.9 %all_gather.19 = bf16[32,2048]{1,0:T(8,128)(2,1)S(1)} all-gather(bf16[16,2048]{1,0:T(8,128)(2,1)S(1)} %convolution_convert_fusion.1), channel_id=1, replica_groups=mesh['dp'=16,'expert'=2] {'expert'}, dimensions={0}, use_global_device_ids=true | all-gather | bytes 196608 | tf_op jit(solution)/shard_map/all_gather | solution.py:48
  20.0 0.0 copy-done
  20.0 0.2 convolution_convert_fusion.2
  20.2 4.9 %all_gather.15 = bf16[32,2048]{1,0:T(8,128)(2,1)S(1)} all-gather(bf16[16,2048]{1,0:T(8,128)(2,1)S(1)} %convolution_convert_fusion.2), channel_id=1, replica_groups=mesh['dp'=16,'expert'=2] {'expert'}, dimensions={0}, use_global_device_ids=true | all-gather | bytes 196608 | tf_op jit(solution)/shard_map/all_gather | solution.py:22
  25.1 29.2 %all-gather.4.cloned.1.call-done = bf16[2048,512]{1,0:T(8,128)(2,1)} async-done(((bf16[128,512]{1,0:T(8,128)(2,1)}), bf16[2048,512]{1,0:T(8,128)(2,1)}) %all-gather.4.cloned.1.call-update) | async-done | bytes 2097168 | tf_op jit(solution)/shard_map/all_gather | solution.py:24
  54.4 2.0 fusion.19
  56.4 40.3 %all-gather.6.cloned.1.call-done = bf16[2048,512]{1,0:T(8,128)(2,1)} async-done(((bf16[128,512]{1,0:T(8,128)(2,1)}), bf16[2048,512]{1,0:T(8,128)(2,1)}) %all-gather.6.cloned.1.call-update) | async-done | bytes 2097168 | tf_op jit(solution)/shard_map/all_gather | solution.py:27
  96.7 2.0 multiply_convert_fusion.2
  98.8 40.3 %all-gather.8.cloned.1.call-done = bf16[2048,512]{1,0:T(8,128)(2,1)} async-done(((bf16[128,512]{1,0:T(8,128)(2,1)}), bf16[2048,512]{1,0:T(8,128)(2,1)}) %all-gather.8.cloned.1.call-update) | async-done | bytes 2097168 | tf_op jit(solution)/shard_map/all_gather | solution.py:31
  139.1 0.0 copy-start.1
  139.1 3.1 %convolution_convert_fusion = bf16[32,2048]{1,0:T(8,128)(2,1)} fusion(bf16[32,512]{1,0:T(8,128)(2,1)S(1)} %get-tuple-element.17, bf16[2048,512]{1,0:T(8,128)(2,1)} %all-gather.8.cloned.1.call-done), kind=kOutput, calls=%fused_computation.6 | convolution fusion | flops 67174400 | bytes 2260992 | tf_op jit(solution)/shard_map/dot_general | solution.py:32
  142.2 0.0 reduce-scatter.3.cloned.1.call-update
  142.3 0.0 reduce-scatter.5.cloned.1.call-start
  142.3 0.7 convolution_multiply_fusion
  143.1 0.0 copy-done.1
  143.1 0.5 fusion.20
  143.5 0.8 convolution_multiply_fusion.1
  144.3 0.8 convolution_multiply_fusion.2
  145.1 5.4 %pad_maximum_fusion = f32[2048,1536]{0,1:T(8,128)} fusion(f32[2048,512]{0,1:T(8,128)S(1)} %convolution_multiply_fusion, f32[2048,512]{0,1:T(8,128)S(1)} %convolution_multiply_fusion.1, f32[2048,512]{0,1:T(8,128)S(1)} %convolution_multiply_fusion.2), kind=kLoop, calls=%fused_computation | loop fusion | flops 6291456 | bytes 25165824 | tf_op jit(solution)/shard_map/concatenate | solution.py:64
  150.5 0.0 reduce-scatter.5.cloned.1.call-update
  150.5 1.0 reduce-scatter.3.cloned.1.call-done
  151.5 2.0 fusion
  153.5 136.7 %reduce-scatter.5.cloned.1.call-done = f32[128,1536]{0,1:T(8,128)} async-done(((f32[2048,1536]{0,1:T(8,128)}), f32[128,1536]{0,1:T(8,128)}) %reduce-scatter.5.cloned.1.call-update) | async-done | bytes 786448 | tf_op jit(solution)/shard_map/reduce_scatter | solution.py:63
  290.2 1.2 convert.6
  291.4 0.8 copy.19
  292.2 0.8 copy.18
  292.9 0.8 copy.17
  (3 shorter events, 0.1 us)
Async XLA Ops:
  7.2 12.9 %copy-start = (bf16[128,2048]{1,0:T(8,128)(2,1)S(1)}, bf16[128,2048]{1,0:T(8,128)(2,1)}, u32[]{:S(2)}) copy-start(bf16[128,2048]{1,0:T(8,128)(2,1)} %param.8) | copy-start | bytes 1572868
  7.2 47.2 %all-gather.4.cloned.1.call-start = ((), (), s32[]{:S(2)}) async-start(), calls=%async_computation.2 | async-start | bytes 2228224 | tf_op jit(solution)/shard_map/all_gather | solution.py:24
  7.9 88.8 %all-gather.6.cloned.1.call-start = ((), (), s32[]{:S(2)}) async-start(), calls=%async_computation.3 | async-start | bytes 2228224 | tf_op jit(solution)/shard_map/all_gather | solution.py:27
  8.7 130.4 %all-gather.8.cloned.1.call-start = ((), (), s32[]{:S(2)}) async-start(), calls=%async_computation.4 | async-start | bytes 2228224 | tf_op jit(solution)/shard_map/all_gather | solution.py:31
  9.4 142.1 %reduce-scatter.3.cloned.1.call-start = ((), (), s32[]{:S(2)}) async-start(), calls=%async_computation.5 | async-start | bytes 196608 | tf_op jit(solution)/shard_map/reduce_scatter | solution.py:33
  139.1 4.0 %copy-start.1 = (bf16[2048,512]{1,0:T(8,128)(2,1)S(1)}, bf16[2048,512]{1,0:T(8,128)(2,1)}, u32[]{:S(2)}) copy-start(bf16[2048,512]{1,0:T(8,128)(2,1)} %all-gather.8.cloned.1.call-done) | copy-start | bytes 6291460
  142.3 147.9 %reduce-scatter.5.cloned.1.call-start = ((), (), s32[]{:S(2)}) async-start(), calls=%async_computation.6 | async-start | bytes 13369344 | tf_op jit(solution)/shard_map/reduce_scatter | solution.py:63
Sparse Core Ops, SparseCore 0:
  10.2 44.1 all-gather.3
  56.5 40.1 all-gather.5
  98.9 40.1 all-gather.7
  142.4 9.0 reduce-scatter.2
  155.4 134.7 reduce-scatter.4
where the time goes:
time: 301 us; the launch traced here: 300 us
  waiting for transfers between devices  250 us (83%)
  between operations  14.5 us (5%)
  matrix products  13.7 us (5%)
  blocking collectives  10.8 us (4%)
  other arithmetic  8.91 us (3%)
    reduce_scatter x1, waiting for transfers between devices, per_device(): lax.psum_scatter(jnp.concatenate([term_of(picked, dgate), term_of(picked,...  137 us
    all_gather x1, waiting for transfers between devices, per_device(): full_down = lax.all_gather(w_down, 'dp', axis=0, tiled=True)  40.3 us
    all_gather x1, waiting for transfers between devices, per_device(): lax.all_gather(w_up, 'dp', axis=0, tiled=True)  40.3 us
    all_gather x1, waiting for transfers between devices, per_device(): lax.all_gather(w_gate, 'dp', axis=0, tiled=True)  29.2 us
  transfers between devices with their start and end apart: 5, of which 5 were waited for; matrix products, arithmetic and copies ran while one was open for 6% of the time, Pallas kernels for 0%

commit v1 on v0

v1 whole, which is shorter than its diff:
```python
import functools

import jax
import jax.numpy as jnp
from jax import lax
from jax.experimental import pallas as pl
from jax.experimental.pallas import tpu as pltpu
from jax.sharding import PartitionSpec as P

F32, BF16 = jnp.float32, jnp.bfloat16
MESH = pl.DeviceIdType.MESH


def dot(a, b, dims):
    return lax.dot_general(a, b, (dims, ((), ())), preferred_element_type=F32)


def kernel(
    pairs, members, cap,
    join, tok, cot, ids, wts, wg, wu, wd,
    mixed, grad_gate, grad_up, grad_down,
    wfull, blk, recv1, send2, recv2, acc, all3, send4, recv4, gacc, sendg, recvg,
    sw, rw, s1, r1, s2, r2, s3, r3, s4, r4, sg, rg,
):
    p, j = lax.axis_index("dp"), lax.axis_index("expert")
    pair, core = lax.div(p, 2), lax.rem(p, 2)
    total = pairs * members
    flat = pair * members + j
    partner = (2 * pair + 1 - core, j)
    tok_count = tok.shape[0]
    depth, width = wg.shape
    chip_depth = 2 * depth
    rows = members * cap

    def flat_peer(d):
        other = lax.rem(flat + d, total)
        return other, lax.div(other, members), lax.rem(other, members)

    def copy(src, dst, send, recv, device):
        return pltpu.make_async_remote_copy(
            src_ref=src, dst_ref=dst, send_sem=send, recv_sem=recv, device_id=device, device_id_type=MESH
        )

    barrier = pltpu.get_barrier_semaphore()

    def greet(d, carry):
        _, pair2, j2 = flat_peer(d)
        pl.semaphore_signal(barrier, inc=1, device_id=(2 * pair2 + core, j2), device_id_type=MESH)
        return carry

    lax.fori_loop(1, total, greet, 0)
    pl.semaphore_signal(barrier, inc=1, device_id=partner, device_id_type=MESH)

    chosen = ids[...] == 0
    routed = jnp.max(jnp.where(chosen, 1.0, 0.0), axis=1, keepdims=True)
    weight = jnp.sum(jnp.where(chosen, wts[...], 0.0), axis=1, keepdims=True)
    lower = lax.broadcasted_iota(jnp.int32, (tok_count, tok_count), 1) <= lax.broadcasted_iota(
        jnp.int32, (tok_count, tok_count), 0
    )
    wide = jnp.broadcast_to(routed, (tok_count, rows))
    places = dot(jnp.where(lower, 1.0, 0.0).astype(BF16), wide.astype(BF16), ((1,), (0,))) - 1.0
    slot = lax.rem(lax.broadcasted_iota(jnp.int32, (tok_count, rows), 1), cap).astype(F32)
    chooser = jnp.where((places == slot) & (wide > 0.5), 1.0, 0.0)
    chooser_half = chooser.astype(BF16)
    pick = chooser.T.astype(BF16)[:cap]
    active = 1.0 - join[p].astype(F32)
    scaled = (cot[...].astype(F32) * (weight * active)).astype(BF16)
    picked_rows = dot(pick, tok[...], ((1,), (0,))).astype(BF16)
    dpicked_rows = dot(pick, scaled, ((1,), (0,))).astype(BF16)
    for q in range(pairs):
        cols = slice(q * chip_depth, (q + 1) * chip_depth)
        blk[q, 0] = picked_rows[:, cols]
        blk[q, 1] = dpicked_rows[:, cols]

    pl.semaphore_wait(barrier, total)

    def start1(d, carry):
        _, pair2, j2 = flat_peer(d)
        copy(blk.at[pair2], recv1.at[flat], s1.at[d], r1.at[d], (2 * pair2 + core, j2)).start()
        return carry

    lax.fori_loop(1, total, start1, 0)
    weights = (wg, wu, wd)
    for n, w in enumerate(weights):
        copy(w, wfull.at[n, core], sw.at[n], rw.at[n], partner).start()
        wfull[n, core] = w[...]
    recv1[flat] = blk[pair]
    for n, w in enumerate(weights):
        copy(w, wfull.at[n, 1 - core], sw.at[n], rw.at[n], partner).wait_recv()

    def wait1(d, carry):
        copy(blk.at[0], recv1.at[lax.rem(flat - d + total, total)], s1.at[d], r1.at[d], partner).wait_recv()
        return carry

    lax.fori_loop(1, total, wait1, 0)

    picked = recv1[:, 0].reshape(total * cap, chip_depth)
    dpicked = recv1[:, 1].reshape(total * cap, chip_depth)
    full = [wfull[n].reshape(chip_depth, width) for n in range(3)]
    for n, left in enumerate((picked, picked, dpicked)):
        send2[:, n] = dot(left, full[n], ((1,), (0,))).astype(BF16).reshape(pairs, rows, width)

    def start2(d, carry):
        pair2 = lax.rem(pair + d, pairs)
        copy(send2.at[pair2], recv2.at[pair], s2.at[d], r2.at[d], (2 * pair2 + core, j)).start()
        return carry

    lax.fori_loop(1, pairs, start2, 0)
    acc[...] = send2[pair].astype(F32)

    def add2(d, carry):
        source = lax.rem(pair - d + pairs, pairs)
        copy(send2.at[0], recv2.at[source], s2.at[d], r2.at[d], partner).wait_recv()
        acc[...] += recv2[source].astype(F32)
        return carry

    lax.fori_loop(1, pairs, add2, 0)

    gate, up, dhidden = acc[0], acc[1], acc[2]
    sig = 1.0 / (1.0 + jnp.exp(-gate))
    all3[pair, 0] = (gate * sig * up).astype(BF16)
    all3[pair, 1] = (dhidden * up * sig * (1.0 + gate * (1.0 - sig))).astype(BF16)
    all3[pair, 2] = (dhidden * gate * sig).astype(BF16)

    def start3(d, carry):
        pair2 = lax.rem(pair + d, pairs)
        copy(all3.at[pair], all3.at[pair], s3.at[d], r3.at[d], (2 * pair2 + core, j)).start()
        return carry

    lax.fori_loop(1, pairs, start3, 0)

    def wait3(d, carry):
        source = lax.rem(pair - d + pairs, pairs)
        copy(all3.at[pair], all3.at[source], s3.at[d], r3.at[d], partner).wait_recv()
        return carry

    lax.fori_loop(1, pairs, wait3, 0)

    hidden, dgate, dup = (all3[:, n].reshape(pairs * rows, width) for n in range(3))
    send4[...] = dot(hidden, full[2], ((1,), (1,))).astype(BF16).reshape(total, cap, chip_depth)

    def start4(d, carry):
        other, pair2, j2 = flat_peer(d)
        copy(send4.at[other], recv4.at[j, pair], s4.at[d], r4.at[d], (2 * pair2 + core, j2)).start()
        return carry

    lax.fori_loop(1, total, start4, 0)
    recv4[j, pair] = send4[flat]

    for n, (left, right) in enumerate(((picked, dgate), (picked, dup), (dpicked, hidden))):
        term = dot(left, right, ((0,), (0,))).reshape(2, depth, width)
        gacc[n] = term
        sendg[n] = term.astype(BF16)
        copy(sendg.at[n, 1 - core], recvg.at[n], sg.at[n], rg.at[n], partner).start()

    def wait4(d, carry):
        source = lax.rem(flat - d + total, total)
        place = recv4.at[lax.rem(source, members), lax.div(source, members)]
        copy(send4.at[0], place, s4.at[d], r4.at[d], partner).wait_recv()
        return carry

    lax.fori_loop(1, total, wait4, 0)
    for q in range(pairs):
        part = recv4[:, q].reshape(rows, chip_depth)
        placed = dot(chooser_half, part, ((1,), (0,))) * weight
        mixed[:, q * chip_depth : (q + 1) * chip_depth] = placed.astype(BF16)

    for n, out in enumerate((grad_gate, grad_up, grad_down)):
        copy(sendg.at[n, 0], recvg.at[n], sg.at[n], rg.at[n], partner).wait_recv()
        out[...] = (gacc[n, core] + recvg[n].astype(F32)).astype(BF16)

    for n, w in enumerate(weights):
        copy(w, wfull.at[n, core], sw.at[n], rw.at[n], partner).wait_send()
        copy(sendg.at[n, 0], recvg.at[n], sg.at[n], rg.at[n], partner).wait_send()

    def drain_flat(d, carry):
        copy(blk.at[0], recv1.at[0], s1.at[d], r1.at[d], partner).wait_send()
        copy(send4.at[0], recv4.at[0, 0], s4.at[d], r4.at[d], partner).wait_send()
        return carry

    def drain_pair(d, carry):
        copy(send2.at[0], recv2.at[0], s2.at[d], r2.at[d], partner).wait_send()
        copy(all3.at[0], all3.at[0], s3.at[d], r3.at[d], partner).wait_send()
        return carry

    lax.fori_loop(1, total, drain_flat, 0)
    lax.fori_loop(1, pairs, drain_pair, 0)


def per_device(pairs, members, tokens, cotangent, expert_ids, route_weights, join_groups, w_gate, w_up, w_down):
    tok_count, model = tokens.shape
    depth, width = w_gate.shape
    cap = tok_count // 8
    total = pairs * members
    rows = members * cap
    vmem = pl.BlockSpec(memory_space=pltpu.VMEM)
    dma = pltpu.SemaphoreType.DMA
    grad = jax.ShapeDtypeStruct((depth, width), BF16)
    return pl.pallas_call(
        functools.partial(kernel, pairs, members, cap),
        out_shape=(jax.ShapeDtypeStruct((tok_count, model), BF16), grad, grad, grad),
        in_specs=[pl.BlockSpec(memory_space=pltpu.SMEM)] + [vmem] * 7,
        out_specs=(vmem,) * 4,
        scratch_shapes=[
            pltpu.VMEM((3, 2, depth, width), BF16),
            pltpu.VMEM((pairs, 2, cap, 2 * depth), BF16),
            pltpu.VMEM((total, 2, cap, 2 * depth), BF16),
            pltpu.VMEM((pairs, 3, rows, width), BF16),
            pltpu.VMEM((pairs, 3, rows, width), BF16),
            pltpu.VMEM((3, rows, width), F32),
            pltpu.VMEM((pairs, 3, rows, width), BF16),
            pltpu.VMEM((total, cap, 2 * depth), BF16),
            pltpu.VMEM((members, pairs, cap, 2 * depth), BF16),
            pltpu.VMEM((3, 2, depth, width), F32),
            pltpu.VMEM((3, 2, depth, width), BF16),
            pltpu.VMEM((3, depth, width), BF16),
            dma((3,)), dma((3,)),
            dma((total,)), dma((total,)),
            dma((pairs,)), dma((pairs,)),
            dma((pairs,)), dma((pairs,)),
            dma((total,)), dma((total,)),
            dma((3,)), dma((3,)),
        ],
        compiler_params=pltpu.CompilerParams(
            collective_id=0, has_side_effects=True, vmem_limit_bytes=48 * 1024 * 1024
        ),
        name="expert_step",
    )(join_groups, tokens, cotangent, expert_ids, route_weights, w_gate, w_up, w_down)


def solution(mesh):
    in_specs = (
        P(("dp", "expert"), None),
        P(("dp", "expert"), None),
        P(("dp", "expert"), None),
        P(("dp", "expert"), None),
        P(),
        P("dp", "expert"),
        P("dp", "expert"),
        P("dp", "expert"),
    )
    out_specs = (P(("dp", "expert"), None), P("dp", "expert"), P("dp", "expert"), P("dp", "expert"))
    body = functools.partial(per_device, mesh.shape["dp"] // 2, mesh.shape["expert"])
    return jax.shard_map(body, mesh=mesh, in_specs=in_specs, out_specs=out_specs, check_vma=False)
```

time: 301 us -> 72 us (0.24)
  waiting for transfers between devices: 250 us -> 0 us
  Pallas kernels: 0 us -> 62.7 us
  between operations: 14.5 us -> 0.68 us
  matrix products: 13.7 us -> 0 us
  blocking collectives: 10.8 us -> 0 us
  other arithmetic: 8.91 us -> 0 us
  local copies, waits for them, and re-layouts: 2.47 us -> 8.27 us
    reduce_scatter x2 -> x0, waiting for transfers between devices: 138 us -> none  [the longest x1 137 us: per_device(): lax.psum_scatter(jnp.concatenate([term_of(picked, dgate), term_of(picked,...]
    all_gather x3 -> x0, waiting for transfers between devices: 110 us -> none  [the longest x1 40.3 us: per_device(): full_down = lax.all_gather(w_down, 'dp', axis=0, tiled=True)]
    pallas_call x0 -> x1, Pallas kernels: none -> 62.7 us  [per_device(): pl.pallas_call(functools.partial(kernel, pairs, members, cap), out_shape=...]
    dot_general x10 -> x0, matrix products: 13.7 us -> none  [the longest x1 3.12 us: per_device(): lax.dot_general(hidden, full_down, trans_dims, preferred_element_type=jnp...]
    all_gather x2 -> x0, blocking collectives: 10.8 us -> none  [the longest x1 5.86 us: per_device(): dpicked = lax.all_gather(dpicked_local, 'expert', axis=0, tiled=True)]
    unnamed x7 -> x18, local copies, waits for them, and re-layouts: 2.32 us -> 8.27 us
    concatenate x1 -> x0, other arithmetic: 5.43 us -> none  [per_device(): jnp.concatenate([term_of(picked, dgate), term_of(picked, dup), term_of(dp...]
  transfers between devices with their start and end apart: 5 -> 0, of which waited for: 5 -> 0; matrix products, arithmetic and copies ran while one was open for 6% -> 0% of each run, Pallas kernels for 0% -> 0%
where the time goes in v1:
time: 72 us; the launch traced here: 71.7 us
  Pallas kernels  62.7 us (87%)
  local copies, waits for them, and re-layouts  8.27 us (11%)
    pallas_call x1, Pallas kernels, per_device(): pl.pallas_call(functools.partial(kernel, pairs, members, cap), out_shape=...  62.7 us
    unnamed x18, local copies, waits for them, and re-layouts  8.27 us

profile of v1, /device:TPU:0, one launch (start us, length us, event | category | flops | bytes accessed | tf_op | source)
XLA Modules:
  0.0 71.7 jit_solution(9202226878224375532)
XLA Ops:
  0.6 0.0 copy-start.2
  0.6 0.8 %copy.12.ids = s32[128,8]{1,0:T(8,128)S(1)} copy(s32[128,8]{0,1:T(8,128)} %param.10) | data formatting | bytes 8192 | tf_op args[2]
  1.5 0.0 copy-start.5
  1.5 0.8 %copy.13.wts = f32[128,8]{1,0:T(8,128)S(1)} copy(f32[128,8]{0,1:T(8,128)} %param.11) | data formatting | bytes 8192 | tf_op args[3]
  2.3 0.0 copy-done.2
  2.3 0.0 copy-done.5
  2.3 0.0 copy-start
  2.3 1.0 %copy-done = bf16[128,2048]{1,0:T(8,128)(2,1)S(1)} copy-done((bf16[128,2048]{1,0:T(8,128)(2,1)S(1)}, bf16[128,2048]{1,0:T(8,128)(2,1)}, u32[]{:S(2)}) %copy-start) | copy-done | bytes 524312
  3.3 0.0 copy-start.1
  3.3 1.0 %copy-done.1 = bf16[128,2048]{1,0:T(8,128)(2,1)S(1)} copy-done((bf16[128,2048]{1,0:T(8,128)(2,1)S(1)}, bf16[128,2048]{1,0:T(8,128)(2,1)}, u32[]{:S(2)}) %copy-start.1) | copy-done | bytes 524312
  4.4 0.0 copy-start.3
  4.4 0.9 %copy-done.3 = bf16[128,512]{1,0:T(8,128)(2,1)S(1)} copy-done((bf16[128,512]{1,0:T(8,128)(2,1)S(1)}, bf16[128,512]{1,0:T(8,128)(2,1)}, u32[]{:S(2)}) %copy-start.3) | copy-done | bytes 131096
  5.3 0.0 copy-start.4
  5.3 0.9 %copy-done.4 = bf16[128,512]{1,0:T(8,128)(2,1)S(1)} copy-done((bf16[128,512]{1,0:T(8,128)(2,1)S(1)}, bf16[128,512]{1,0:T(8,128)(2,1)}, u32[]{:S(2)}) %copy-start.4) | copy-done | bytes 131096
  6.2 62.7 %expert_step.1 = (bf16[128,2048]{1,0:T(8,128)(2,1)S(1)}, bf16[128,512]{1,0:T(8,128)(2,1)S(1)}, bf16[128,512]{1,0:T(8,128)(2,1)S(1)}, bf16[128,512]{1,0:T(8,128)(2,1)S(1)}) custom-call(s32[16]{0:T(128)S(1)} %copy-done.5, bf16[128,2048]{1,0:T(8,128)(2,1)S(1)} %copy-done, bf16[128,2048]{1,0:T(8,128)(2,1)S(1)} %copy-done.1, s32[128,8]{1,0:T(8,128)S(1)} %copy.12.ids, ...), custom_call_target="tpu_custom_call" | custom-call | tf_op jit(solution)/shard_map/expert_step/pallas_call | solution.py:199
  68.9 0.8 %copy.18 = bf16[128,2048]{1,0:T(8,128)(2,1)} copy(bf16[128,2048]{1,0:T(8,128)(2,1)S(1)} %get-tuple-element.8) | data formatting | bytes 1048576
  69.7 0.7 copy.19
  70.4 0.7 copy.20
  71.0 0.7 copy.21
Async XLA Ops:
  0.6 1.6 %copy-start.2 = (bf16[128,512]{1,0:T(8,128)(2,1)S(1)}, bf16[128,512]{1,0:T(8,128)(2,1)}, u32[]{:S(2)}) copy-start(bf16[128,512]{1,0:T(8,128)(2,1)} %wg.1) | copy-start | bytes 393220
  1.5 0.8 %copy-start.5 = (s32[16]{0:T(128)S(1)}, s32[16]{0:T(128)}, u32[]{:S(2)}) copy-start(s32[16]{0:T(128)} %join.1) | copy-start | bytes 196
  2.3 1.0 %copy-start = (bf16[128,2048]{1,0:T(8,128)(2,1)S(1)}, bf16[128,2048]{1,0:T(8,128)(2,1)}, u32[]{:S(2)}) copy-start(bf16[128,2048]{1,0:T(8,128)(2,1)} %tok.1) | copy-start | bytes 1572868
  3.3 1.0 %copy-start.1 = (bf16[128,2048]{1,0:T(8,128)(2,1)S(1)}, bf16[128,2048]{1,0:T(8,128)(2,1)}, u32[]{:S(2)}) copy-start(bf16[128,2048]{1,0:T(8,128)(2,1)} %cot.1) | copy-start | bytes 1572868
  4.4 0.9 %copy-start.3 = (bf16[128,512]{1,0:T(8,128)(2,1)S(1)}, bf16[128,512]{1,0:T(8,128)(2,1)}, u32[]{:S(2)}) copy-start(bf16[128,512]{1,0:T(8,128)(2,1)} %wu.1) | copy-start | bytes 393220
  5.3 0.9 %copy-start.4 = (bf16[128,512]{1,0:T(8,128)(2,1)S(1)}, bf16[128,512]{1,0:T(8,128)(2,1)}, u32[]{:S(2)}) copy-start(bf16[128,512]{1,0:T(8,128)(2,1)} %wd.1) | copy-start | bytes 393220

commit v2 on v1

--- a/solution.py
+++ b/solution.py
@@ -19,14 +19,18 @@
     pairs, members, cap,
     join, tok, cot, ids, wts, wg, wu, wd,
     mixed, grad_gate, grad_up, grad_down,
-    wfull, blk, recv1, send2, recv2, acc, all3, send4, recv4, gacc, sendg, recvg,
-    sw, rw, s1, r1, s2, r2, s3, r3, s4, r4, sg, rg,
+    tokv, cotv, wfull, blk, recv1, part, send2, recv_y, mid, recv_z, acc, all3, send4, recv4, gacc, sendg, recvg,
+    local, sw, rw, s1, r1, s2y, r2y, s2z, r2z, s3y, r3y, s3z, r3z, s4, r4, sg, rg,
 ):
     p, j = lax.axis_index("dp"), lax.axis_index("expert")
     pair, core = lax.div(p, 2), lax.rem(p, 2)
     total = pairs * members
     flat = pair * members + j
     partner = (2 * pair + 1 - core, j)
+    line, side = lax.div(pair, 2), lax.rem(pair, 2)
+    lines = pairs // 2
+    across = (2 * (2 * line + 1 - side) + core, j)
+    last = lines - 1
     tok_count = tok.shape[0]
     depth, width = wg.shape
     chip_depth = 2 * depth
@@ -41,6 +45,15 @@
             src_ref=src, dst_ref=dst, send_sem=send, recv_sem=recv, device_id=device, device_id_type=MESH
         )
 
+    def on_line(other):
+        return (2 * (2 * other + side) + core, j)
+
+    weights = (wg, wu, wd)
+    loads = [(cot, cotv), (tok, tokv)] + [(w, wfull.at[n, core]) for n, w in enumerate(weights)]
+    loads = [pltpu.make_async_copy(src, dst, local.at[n]) for n, (src, dst) in enumerate(loads)]
+    for load in loads:
+        load.start()
+
     barrier = pltpu.get_barrier_semaphore()
 
     def greet(d, carry):
@@ -52,21 +65,23 @@
     pl.semaphore_signal(barrier, inc=1, device_id=partner, device_id_type=MESH)
 
     chosen = ids[...] == 0
-    routed = jnp.max(jnp.where(chosen, 1.0, 0.0), axis=1, keepdims=True)
-    weight = jnp.sum(jnp.where(chosen, wts[...], 0.0), axis=1, keepdims=True)
-    lower = lax.broadcasted_iota(jnp.int32, (tok_count, tok_count), 1) <= lax.broadcasted_iota(
-        jnp.int32, (tok_count, tok_count), 0
+    routed = jnp.max(jnp.where(chosen, 1.0, 0.0), axis=0, keepdims=True)
+    weight = jnp.sum(jnp.where(chosen, wts[...], 0.0), axis=0, keepdims=True)
+    upper = lax.broadcasted_iota(jnp.int32, (tok_count, tok_count), 0) <= lax.broadcasted_iota(
+        jnp.int32, (tok_count, tok_count), 1
     )
-    wide = jnp.broadcast_to(routed, (tok_count, rows))
-    places = dot(jnp.where(lower, 1.0, 0.0).astype(BF16), wide.astype(BF16), ((1,), (0,))) - 1.0
-    slot = lax.rem(lax.broadcasted_iota(jnp.int32, (tok_count, rows), 1), cap).astype(F32)
-    chooser = jnp.where((places == slot) & (wide > 0.5), 1.0, 0.0)
-    chooser_half = chooser.astype(BF16)
-    pick = chooser.T.astype(BF16)[:cap]
+    wide = jnp.broadcast_to(routed, (cap, tok_count))
+    places = dot(wide.astype(BF16), jnp.where(upper, 1.0, 0.0).astype(BF16), ((1,), (0,))) - 1.0
+    slot = lax.broadcasted_iota(jnp.int32, (cap, tok_count), 0).astype(F32)
+    pick = jnp.where((places == slot) & (wide > 0.5), 1.0, 0.0)
+    slot_weight = jnp.sum(pick * weight, axis=1, keepdims=True)
+    spread = pick.T.astype(BF16)
+    pick = pick.astype(BF16)
     active = 1.0 - join[p].astype(F32)
-    scaled = (cot[...].astype(F32) * (weight * active)).astype(BF16)
-    picked_rows = dot(pick, tok[...], ((1,), (0,))).astype(BF16)
-    dpicked_rows = dot(pick, scaled, ((1,), (0,))).astype(BF16)
+    loads[0].wait()
+    dpicked_rows = (dot(pick, cotv[...], ((1,), (0,))) * (slot_weight * active)).astype(BF16)
+    loads[1].wait()
+    picked_rows = dot(pick, tokv[...], ((1,), (0,))).astype(BF16)
     for q in range(pairs):
         cols = slice(q * chip_depth, (q + 1) * chip_depth)
         blk[q, 0] = picked_rows[:, cols]
@@ -80,12 +95,11 @@
         return carry
 
     lax.fori_loop(1, total, start1, 0)
-    weights = (wg, wu, wd)
     for n, w in enumerate(weights):
         copy(w, wfull.at[n, core], sw.at[n], rw.at[n], partner).start()
-        wfull[n, core] = w[...]
     recv1[flat] = blk[pair]
     for n, w in enumerate(weights):
+        loads[2 + n].wait()
         copy(w, wfull.at[n, 1 - core], sw.at[n], rw.at[n], partner).wait_recv()
 
     def wait1(d, carry):
@@ -98,23 +112,35 @@
     dpicked = recv1[:, 1].reshape(total * cap, chip_depth)
     full = [wfull[n].reshape(chip_depth, width) for n in range(3)]
     for n, left in enumerate((picked, picked, dpicked)):
-        send2[:, n] = dot(left, full[n], ((1,), (0,))).astype(BF16).reshape(pairs, rows, width)
+        term = dot(left, full[n], ((1,), (0,))).reshape(pairs, rows, width)
+        part[:, n] = term
+        send2[:, n] = term.astype(BF16)
 
     def start2(d, carry):
-        pair2 = lax.rem(pair + d, pairs)
-        copy(send2.at[pair2], recv2.at[pair], s2.at[d], r2.at[d], (2 * pair2 + core, j)).start()
-        return carry
-
-    lax.fori_loop(1, pairs, start2, 0)
-    acc[...] = send2[pair].astype(F32)
+        other = lax.rem(line + 1 + d, lines)
+        copy(send2.at[2 * other + 1 - side], recv_y.at[other], s2y.at[d], r2y.at[d], across).start()
+        return carry
+
+    lax.fori_loop(0, lines, start2, 0)
+
+    def pass2(d, carry):
+        other = lax.rem(line + 1 + d, lines)
+        copy(send2.at[0], recv_y.at[other], s2y.at[d], r2y.at[d], across).wait_recv()
+        mid[other] = (part[2 * other + side] + recv_y[other].astype(F32)).astype(BF16)
+        copy(mid.at[other], recv_z.at[line], s2z.at[d], r2z.at[d], on_line(other)).start()
+        return carry
+
+    lax.fori_loop(0, last, pass2, 0)
+    copy(send2.at[0], recv_y.at[line], s2y.at[last], r2y.at[last], across).wait_recv()
+    acc[...] = part[pair] + recv_y[line].astype(F32)
 
     def add2(d, carry):
-        source = lax.rem(pair - d + pairs, pairs)
-        copy(send2.at[0], recv2.at[source], s2.at[d], r2.at[d], partner).wait_recv()
-        acc[...] += recv2[source].astype(F32)
-        return carry
-
-    lax.fori_loop(1, pairs, add2, 0)
+        source = lax.rem(line + last - d, lines)
+        copy(mid.at[0], recv_z.at[source], s2z.at[d], r2z.at[d], across).wait_recv()
+        acc[...] += recv_z[source].astype(F32)
+        return carry
+
+    lax.fori_loop(0, last, add2, 0)
 
     gate, up, dhidden = acc[0], acc[1], acc[2]
     sig = 1.0 / (1.0 + jnp.exp(-gate))
@@ -122,19 +148,31 @@
     all3[pair, 1] = (dhidden * up * sig * (1.0 + gate * (1.0 - sig))).astype(BF16)
     all3[pair, 2] = (dhidden * gate * sig).astype(BF16)
 
+    copy(all3.at[pair], all3.at[pair], s3y.at[last], r3y.at[last], across).start()
+
     def start3(d, carry):
-        pair2 = lax.rem(pair + d, pairs)
-        copy(all3.at[pair], all3.at[pair], s3.at[d], r3.at[d], (2 * pair2 + core, j)).start()
-        return carry
-
-    lax.fori_loop(1, pairs, start3, 0)
+        other = lax.rem(line + 1 + d, lines)
+        copy(all3.at[pair], all3.at[pair], s3z.at[d], r3z.at[d], on_line(other)).start()
+        return carry
+
+    lax.fori_loop(0, last, start3, 0)
+
+    def pass3(d, carry):
+        held = all3.at[2 * lax.rem(line + last - d, lines) + side]
+        copy(all3.at[pair], held, s3z.at[d], r3z.at[d], across).wait_recv()
+        copy(held, held, s3y.at[d], r3y.at[d], across).start()
+        return carry
+
+    lax.fori_loop(0, last, pass3, 0)
 
     def wait3(d, carry):
-        source = lax.rem(pair - d + pairs, pairs)
-        copy(all3.at[pair], all3.at[source], s3.at[d], r3.at[d], partner).wait_recv()
-        return carry
-
-    lax.fori_loop(1, pairs, wait3, 0)
+        source = lax.rem(line + last - d, lines)
+        place = all3.at[2 * source + 1 - side]
+        copy(all3.at[pair], place, s3y.at[d], r3y.at[d], across).wait_recv()
+        return carry
+
+    lax.fori_loop(0, last, wait3, 0)
+    copy(all3.at[pair], all3.at[2 * line + 1 - side], s3y.at[last], r3y.at[last], across).wait_recv()
 
     hidden, dgate, dup = (all3[:, n].reshape(pairs * rows, width) for n in range(3))
     send4[...] = dot(hidden, full[2], ((1,), (1,))).astype(BF16).reshape(total, cap, chip_depth)
@@ -161,8 +199,10 @@
 
     lax.fori_loop(1, total, wait4, 0)
     for q in range(pairs):
-        part = recv4[:, q].reshape(rows, chip_depth)
-        placed = dot(chooser_half, part, ((1,), (0,))) * weight
+        out_rows = recv4[0, q].astype(F32)
+        for m in range(1, members):
+            out_rows += recv4[m, q].astype(F32)
+        placed = dot(spread, (out_rows * slot_weight).astype(BF16), ((1,), (0,)))
         mixed[:, q * chip_depth : (q + 1) * chip_depth] = placed.astype(BF16)
 
     for n, out in enumerate((grad_gate, grad_up, grad_down)):
@@ -178,13 +218,19 @@
         copy(send4.at[0], recv4.at[0, 0], s4.at[d], r4.at[d], partner).wait_send()
         return carry
 
-    def drain_pair(d, carry):
-        copy(send2.at[0], recv2.at[0], s2.at[d], r2.at[d], partner).wait_send()
-        copy(all3.at[0], all3.at[0], s3.at[d], r3.at[d], partner).wait_send()
+    def drain_y(d, carry):
+        copy(send2.at[0], recv_y.at[0], s2y.at[d], r2y.at[d], across).wait_send()
+        copy(all3.at[0], all3.at[0], s3y.at[d], r3y.at[d], across).wait_send()
+        return carry
+
+    def drain_z(d, carry):
+        copy(mid.at[0], recv_z.at[0], s2z.at[d], r2z.at[d], across).wait_send()
+        copy(all3.at[0], all3.at[0], s3z.at[d], r3z.at[d], across).wait_send()
         return carry
 
     lax.fori_loop(1, total, drain_flat, 0)
-    lax.fori_loop(1, pairs, drain_pair, 0)
+    lax.fori_loop(0, lines, drain_y, 0)
+    lax.fori_loop(0, last, drain_z, 0)
 
 
 def per_device(pairs, members, tokens, cotangent, expert_ids, route_weights, join_groups, w_gate, w_up, w_down):
@@ -194,19 +240,26 @@
     total = pairs * members
     rows = members * cap
     vmem = pl.BlockSpec(memory_space=pltpu.VMEM)
+    hbm = pl.BlockSpec(memory_space=pl.ANY)
+    lines = pairs // 2
     dma = pltpu.SemaphoreType.DMA
     grad = jax.ShapeDtypeStruct((depth, width), BF16)
     return pl.pallas_call(
         functools.partial(kernel, pairs, members, cap),
         out_shape=(jax.ShapeDtypeStruct((tok_count, model), BF16), grad, grad, grad),
-        in_specs=[pl.BlockSpec(memory_space=pltpu.SMEM)] + [vmem] * 7,
+        in_specs=[pl.BlockSpec(memory_space=pltpu.SMEM), hbm, hbm, vmem, vmem, hbm, hbm, hbm],
         out_specs=(vmem,) * 4,
         scratch_shapes=[
+            pltpu.VMEM((tok_count, model), BF16),
+            pltpu.VMEM((tok_count, model), BF16),
             pltpu.VMEM((3, 2, depth, width), BF16),
             pltpu.VMEM((pairs, 2, cap, 2 * depth), BF16),
             pltpu.VMEM((total, 2, cap, 2 * depth), BF16),
+            pltpu.VMEM((pairs, 3, rows, width), F32),
             pltpu.VMEM((pairs, 3, rows, width), BF16),
-            pltpu.VMEM((pairs, 3, rows, width), BF16),
+            pltpu.VMEM((lines, 3, rows, width), BF16),
+            pltpu.VMEM((lines, 3, rows, width), BF16),
+            pltpu.VMEM((lines, 3, rows, width), BF16),
             pltpu.VMEM((3, rows, width), F32),
             pltpu.VMEM((pairs, 3, rows, width), BF16),
             pltpu.VMEM((total, cap, 2 * depth), BF16),
@@ -214,18 +267,21 @@
             pltpu.VMEM((3, 2, depth, width), F32),
             pltpu.VMEM((3, 2, depth, width), BF16),
             pltpu.VMEM((3, depth, width), BF16),
+            dma((5,)),
             dma((3,)), dma((3,)),
             dma((total,)), dma((total,)),
-            dma((pairs,)), dma((pairs,)),
-            dma((pairs,)), dma((pairs,)),
+            dma((lines,)), dma((lines,)),
+            dma((lines,)), dma((lines,)),
+            dma((lines,)), dma((lines,)),
+            dma((lines,)), dma((lines,)),
             dma((total,)), dma((total,)),
             dma((3,)), dma((3,)),
         ],
         compiler_params=pltpu.CompilerParams(
-            collective_id=0, has_side_effects=True, vmem_limit_bytes=48 * 1024 * 1024
+            collective_id=0, has_side_effects=True, vmem_limit_bytes=60 * 1024 * 1024
         ),
         name="expert_step",
-    )(join_groups, tokens, cotangent, expert_ids, route_weights, w_gate, w_up, w_down)
+    )(join_groups, tokens, cotangent, expert_ids.T, route_weights.T, w_gate, w_up, w_down)
 
 
 def solution(mesh):

time: 72 us -> 55.3 us (0.77)
  Pallas kernels: 62.7 us -> 50 us
  local copies, waits for them, and re-layouts: 8.27 us -> 4.48 us
    pallas_call x1, Pallas kernels: 62.7 us -> 50 us  [per_device(): pl.pallas_call(functools.partial(kernel, pairs, members, cap), out_shape=...]
    unnamed x18 -> x10, local copies, waits for them, and re-layouts: 8.27 us -> 4.48 us
where the time goes in v2:
time: 55.3 us; the launch traced here: 55.1 us
  Pallas kernels  50 us (90%)
  local copies, waits for them, and re-layouts  4.48 us (8%)
  between operations  0.65 us (1%)
    pallas_call x1, Pallas kernels, per_device(): pl.pallas_call(functools.partial(kernel, pairs, members, cap), out_shape=...  50 us
    unnamed x10, local copies, waits for them, and re-layouts  4.48 us

profile of v2, /device:TPU:0, one launch (start us, length us, event | category | flops | bytes accessed | tf_op | source)
XLA Modules:
  0.0 55.1 jit_solution(9825147215724966406)
XLA Ops:
  0.6 50.0 %expert_step.1 = (bf16[128,2048]{1,0:T(8,128)(2,1)}, bf16[128,512]{1,0:T(8,128)(2,1)}, bf16[128,512]{1,0:T(8,128)(2,1)}, bf16[128,512]{1,0:T(8,128)(2,1)}) custom-call(s32[16]{0:T(128)} %join.1, bf16[128,2048]{1,0:T(8,128)(2,1)} %tok.1, bf16[128,2048]{1,0:T(8,128)(2,1)} %cot.1, s32[8,128]{1,0:T(8,128)} %bitcast.2, f32[8,128]{1,0:T(8,128)} %bitcast.3, ...), custom_call_target="tpu_custom_call" | custom-call | tf_op jit(solution)/shard_map/expert_step/pallas_call | solution.py:247
  50.6 0.0 copy-start.2
  50.6 1.9 %copy.16 = bf16[128,2048]{1,0:T(8,128)(2,1)} copy(bf16[128,2048]{1,0:T(8,128)(2,1)} %get-tuple-element.8) | data formatting | bytes 1048576
  52.5 0.0 copy-done.2
  52.5 0.0 copy-start.1
  52.5 0.7 %copy.17 = bf16[128,512]{1,0:T(8,128)(2,1)} copy(bf16[128,512]{1,0:T(8,128)(2,1)S(1)} %copy-done.2) | data formatting | bytes 262144
  53.2 0.3 copy-done.1
  53.5 0.0 copy-start
  53.5 0.7 %copy.18 = bf16[128,512]{1,0:T(8,128)(2,1)} copy(bf16[128,512]{1,0:T(8,128)(2,1)S(1)} %copy-done.1) | data formatting | bytes 262144
  54.1 0.3 copy-done
  54.4 0.7 %copy.19 = bf16[128,512]{1,0:T(8,128)(2,1)} copy(bf16[128,512]{1,0:T(8,128)(2,1)S(1)} %copy-done) | data formatting | bytes 262144
Async XLA Ops:
  50.6 1.9 %copy-start.2 = (bf16[128,512]{1,0:T(8,128)(2,1)S(1)}, bf16[128,512]{1,0:T(8,128)(2,1)}, u32[]{:S(2)}) copy-start(bf16[128,512]{1,0:T(8,128)(2,1)} %get-tuple-element.9) | copy-start | bytes 393220
  52.5 1.0 %copy-start.1 = (bf16[128,512]{1,0:T(8,128)(2,1)S(1)}, bf16[128,512]{1,0:T(8,128)(2,1)}, u32[]{:S(2)}) copy-start(bf16[128,512]{1,0:T(8,128)(2,1)} %get-tuple-element.10) | copy-start | bytes 393220
  53.5 1.0 %copy-start = (bf16[128,512]{1,0:T(8,128)(2,1)S(1)}, bf16[128,512]{1,0:T(8,128)(2,1)}, u32[]{:S(2)}) copy-start(bf16[128,512]{1,0:T(8,128)(2,1)} %get-tuple-element.11) | copy-start | bytes 393220

commit v3 on v2

--- a/solution.py
+++ b/solution.py
@@ -9,6 +9,7 @@
 
 F32, BF16 = jnp.float32, jnp.bfloat16
 MESH = pl.DeviceIdType.MESH
+CHUNKS = 2
 
 
 def dot(a, b, dims):
@@ -112,69 +113,75 @@
     dpicked = recv1[:, 1].reshape(total * cap, chip_depth)
     full = [wfull[n].reshape(chip_depth, width) for n in range(3)]
     for n, left in enumerate((picked, picked, dpicked)):
-        term = dot(left, full[n], ((1,), (0,))).reshape(pairs, rows, width)
-        part[:, n] = term
-        send2[:, n] = term.astype(BF16)
-
-    def start2(d, carry):
-        other = lax.rem(line + 1 + d, lines)
-        copy(send2.at[2 * other + 1 - side], recv_y.at[other], s2y.at[d], r2y.at[d], across).start()
-        return carry
-
-    lax.fori_loop(0, lines, start2, 0)
-
-    def pass2(d, carry):
-        other = lax.rem(line + 1 + d, lines)
-        copy(send2.at[0], recv_y.at[other], s2y.at[d], r2y.at[d], across).wait_recv()
-        mid[other] = (part[2 * other + side] + recv_y[other].astype(F32)).astype(BF16)
-        copy(mid.at[other], recv_z.at[line], s2z.at[d], r2z.at[d], on_line(other)).start()
-        return carry
-
-    lax.fori_loop(0, last, pass2, 0)
-    copy(send2.at[0], recv_y.at[line], s2y.at[last], r2y.at[last], across).wait_recv()
-    acc[...] = part[pair] + recv_y[line].astype(F32)
-
-    def add2(d, carry):
-        source = lax.rem(line + last - d, lines)
-        copy(mid.at[0], recv_z.at[source], s2z.at[d], r2z.at[d], across).wait_recv()
-        acc[...] += recv_z[source].astype(F32)
-        return carry
-
-    lax.fori_loop(0, last, add2, 0)
-
-    gate, up, dhidden = acc[0], acc[1], acc[2]
-    sig = 1.0 / (1.0 + jnp.exp(-gate))
-    all3[pair, 0] = (gate * sig * up).astype(BF16)
-    all3[pair, 1] = (dhidden * up * sig * (1.0 + gate * (1.0 - sig))).astype(BF16)
-    all3[pair, 2] = (dhidden * gate * sig).astype(BF16)
-
-    copy(all3.at[pair], all3.at[pair], s3y.at[last], r3y.at[last], across).start()
-
-    def start3(d, carry):
-        other = lax.rem(line + 1 + d, lines)
-        copy(all3.at[pair], all3.at[pair], s3z.at[d], r3z.at[d], on_line(other)).start()
-        return carry
-
-    lax.fori_loop(0, last, start3, 0)
-
-    def pass3(d, carry):
-        held = all3.at[2 * lax.rem(line + last - d, lines) + side]
-        copy(all3.at[pair], held, s3z.at[d], r3z.at[d], across).wait_recv()
-        copy(held, held, s3y.at[d], r3y.at[d], across).start()
-        return carry
-
-    lax.fori_loop(0, last, pass3, 0)
-
-    def wait3(d, carry):
-        source = lax.rem(line + last - d, lines)
-        place = all3.at[2 * source + 1 - side]
-        copy(all3.at[pair], place, s3y.at[d], r3y.at[d], across).wait_recv()
-        return carry
-
-    lax.fori_loop(0, last, wait3, 0)
-    copy(all3.at[pair], all3.at[2 * line + 1 - side], s3y.at[last], r3y.at[last], across).wait_recv()
-
-    hidden, dgate, dup = (all3[:, n].reshape(pairs * rows, width) for n in range(3))
+        term = dot(left, full[n], ((1,), (0,))).reshape(pairs, CHUNKS, rows // CHUNKS, width)
+        for h in range(CHUNKS):
+            part[h, :, n] = term[:, h]
+            send2[h, :, n] = term[:, h].astype(BF16)
+
+    def start2(h, d, carry):
+        other, at = lax.rem(line + 1 + d, lines), h * lines + d
+        copy(send2.at[h, 2 * other + 1 - side], recv_y.at[h, other], s2y.at[at], r2y.at[at], across).start()
+        return carry
+
+    def pass2(h, d, carry):
+        other, at = lax.rem(line + 1 + d, lines), h * lines + d
+        copy(send2.at[h, 0], recv_y.at[h, other], s2y.at[at], r2y.at[at], across).wait_recv()
+        mid[h, other] = (part[h, 2 * other + side] + recv_y[h, other].astype(F32)).astype(BF16)
+        copy(mid.at[h, other], recv_z.at[h, line], s2z.at[at], r2z.at[at], on_line(other)).start()
+        return carry
+
+    def add2(h, d, carry):
+        source, at = lax.rem(line + last - d, lines), h * lines + d
+        copy(mid.at[h, 0], recv_z.at[h, source], s2z.at[at], r2z.at[at], across).wait_recv()
+        acc[h] += recv_z[h, source].astype(F32)
+        return carry
+
+    def start3(h, d, carry):
+        other, at = lax.rem(line + 1 + d, lines), h * lines + d
+        copy(all3.at[h, pair], all3.at[h, pair], s3z.at[at], r3z.at[at], on_line(other)).start()
+        return carry
+
+    def pass3(h, d, carry):
+        at = h * lines + d
+        held = all3.at[h, 2 * lax.rem(line + last - d, lines) + side]
+        copy(all3.at[h, pair], held, s3z.at[at], r3z.at[at], across).wait_recv()
+        copy(held, held, s3y.at[at], r3y.at[at], across).start()
+        return carry
+
+    def wait3(h, d, carry):
+        at = h * lines + d
+        place = all3.at[h, 2 * lax.rem(line + last - d, lines) + 1 - side]
+        copy(all3.at[h, pair], place, s3y.at[at], r3y.at[at], across).wait_recv()
+        return carry
+
+    for h in range(CHUNKS):
+        lax.fori_loop(0, lines, functools.partial(start2, h), 0)
+    for h in range(CHUNKS):
+        lax.fori_loop(0, last, functools.partial(pass2, h), 0)
+        at = h * lines + last
+        copy(send2.at[h, 0], recv_y.at[h, line], s2y.at[at], r2y.at[at], across).wait_recv()
+        acc[h] = part[h, pair] + recv_y[h, line].astype(F32)
+    for h in range(CHUNKS):
+        lax.fori_loop(0, last, functools.partial(add2, h), 0)
+        gate, up, dhidden = acc[h, 0], acc[h, 1], acc[h, 2]
+        sig = 1.0 / (1.0 + jnp.exp(-gate))
+        all3[h, pair, 0] = (gate * sig * up).astype(BF16)
+        all3[h, pair, 1] = (dhidden * up * sig * (1.0 + gate * (1.0 - sig))).astype(BF16)
+        all3[h, pair, 2] = (dhidden * gate * sig).astype(BF16)
+        lax.fori_loop(0, last, functools.partial(start3, h), 0)
+        at = h * lines + last
+        copy(all3.at[h, pair], all3.at[h, pair], s3y.at[at], r3y.at[at], across).start()
+    for h in range(CHUNKS):
+        lax.fori_loop(0, last, functools.partial(pass3, h), 0)
+    for h in range(CHUNKS):
+        at = h * lines + last
+        place = all3.at[h, 2 * line + 1 - side]
+        copy(all3.at[h, pair], place, s3y.at[at], r3y.at[at], across).wait_recv()
+        lax.fori_loop(0, last, functools.partial(wait3, h), 0)
+
+    hidden, dgate, dup = (
+        jnp.stack([all3[h, :, n] for h in range(CHUNKS)], axis=1).reshape(pairs * rows, width) for n in range(3)
+    )
     send4[...] = dot(hidden, full[2], ((1,), (1,))).astype(BF16).reshape(total, cap, chip_depth)
 
     def start4(d, carry):
@@ -219,18 +226,20 @@
         return carry
 
     def drain_y(d, carry):
-        copy(send2.at[0], recv_y.at[0], s2y.at[d], r2y.at[d], across).wait_send()
-        copy(all3.at[0], all3.at[0], s3y.at[d], r3y.at[d], across).wait_send()
-        return carry
-
-    def drain_z(d, carry):
-        copy(mid.at[0], recv_z.at[0], s2z.at[d], r2z.at[d], across).wait_send()
-        copy(all3.at[0], all3.at[0], s3z.at[d], r3z.at[d], across).wait_send()
+        copy(send2.at[0, 0], recv_y.at[0, 0], s2y.at[d], r2y.at[d], across).wait_send()
+        copy(all3.at[0, 0], all3.at[0, 0], s3y.at[d], r3y.at[d], across).wait_send()
+        return carry
+
+    def drain_z(h, d, carry):
+        at = h * lines + d
+        copy(mid.at[0, 0], recv_z.at[0, 0], s2z.at[at], r2z.at[at], across).wait_send()
+        copy(all3.at[0, 0], all3.at[0, 0], s3z.at[at], r3z.at[at], across).wait_send()
         return carry
 
     lax.fori_loop(1, total, drain_flat, 0)
-    lax.fori_loop(0, lines, drain_y, 0)
-    lax.fori_loop(0, last, drain_z, 0)
+    lax.fori_loop(0, CHUNKS * lines, drain_y, 0)
+    for h in range(CHUNKS):
+        lax.fori_loop(0, last, functools.partial(drain_z, h), 0)
 
 
 def per_device(pairs, members, tokens, cotangent, expert_ids, route_weights, join_groups, w_gate, w_up, w_down):
@@ -255,13 +264,13 @@
             pltpu.VMEM((3, 2, depth, width), BF16),
             pltpu.VMEM((pairs, 2, cap, 2 * depth), BF16),
             pltpu.VMEM((total, 2, cap, 2 * depth), BF16),
-            pltpu.VMEM((pairs, 3, rows, width), F32),
-            pltpu.VMEM((pairs, 3, rows, width), BF16),
-            pltpu.VMEM((lines, 3, rows, width), BF16),
-            pltpu.VMEM((lines, 3, rows, width), BF16),
-            pltpu.VMEM((lines, 3, rows, width), BF16),
-            pltpu.VMEM((3, rows, width), F32),
-            pltpu.VMEM((pairs, 3, rows, width), BF16),
+            pltpu.VMEM((CHUNKS, pairs, 3, rows // CHUNKS, width), F32),
+            pltpu.VMEM((CHUNKS, pairs, 3, rows // CHUNKS, width), BF16),
+            pltpu.VMEM((CHUNKS, lines, 3, rows // CHUNKS, width), BF16),
+            pltpu.VMEM((CHUNKS, lines, 3, rows // CHUNKS, width), BF16),
+            pltpu.VMEM((CHUNKS, lines, 3, rows // CHUNKS, width), BF16),
+            pltpu.VMEM((CHUNKS, 3, rows // CHUNKS, width), F32),
+            pltpu.VMEM((CHUNKS, pairs, 3, rows // CHUNKS, width), BF16),
             pltpu.VMEM((total, cap, 2 * depth), BF16),
             pltpu.VMEM((members, pairs, cap, 2 * depth), BF16),
             pltpu.VMEM((3, 2, depth, width), F32),
@@ -270,10 +279,10 @@
             dma((5,)),
             dma((3,)), dma((3,)),
             dma((total,)), dma((total,)),
-            dma((lines,)), dma((lines,)),
-            dma((lines,)), dma((lines,)),
-            dma((lines,)), dma((lines,)),
-            dma((lines,)), dma((lines,)),
+            dma((CHUNKS * lines,)), dma((CHUNKS * lines,)),
+            dma((CHUNKS * lines,)), dma((CHUNKS * lines,)),
+            dma((CHUNKS * lines,)), dma((CHUNKS * lines,)),
+            dma((CHUNKS * lines,)), dma((CHUNKS * lines,)),
             dma((total,)), dma((total,)),
             dma((3,)), dma((3,)),
         ],

time: 55.3 us -> 55.2 us (level)
  no operation moved by 1% of the time
where the time goes in v3:
time: 55.2 us; the launch traced here: 55 us
  Pallas kernels  49.9 us (90%)
  local copies, waits for them, and re-layouts  4.48 us (8%)
  between operations  0.65 us (1%)
    pallas_call x1, Pallas kernels, per_device(): pl.pallas_call(functools.partial(kernel, pairs, members, cap), out_shape=...  49.9 us
    unnamed x10, local copies, waits for them, and re-layouts  4.48 us

profile of v3, /device:TPU:0, one launch (start us, length us, event | category | flops | bytes accessed | tf_op | source)
XLA Modules:
  0.0 55.0 jit_solution(11978755348898964627)
XLA Ops:
  0.6 49.9 %expert_step.1 = (bf16[128,2048]{1,0:T(8,128)(2,1)}, bf16[128,512]{1,0:T(8,128)(2,1)}, bf16[128,512]{1,0:T(8,128)(2,1)}, bf16[128,512]{1,0:T(8,128)(2,1)}) custom-call(s32[16]{0:T(128)} %join.1, bf16[128,2048]{1,0:T(8,128)(2,1)} %tok.1, bf16[128,2048]{1,0:T(8,128)(2,1)} %cot.1, s32[8,128]{1,0:T(8,128)} %bitcast.2, f32[8,128]{1,0:T(8,128)} %bitcast.3, ...), custom_call_target="tpu_custom_call" | custom-call | tf_op jit(solution)/shard_map/expert_step/pallas_call | solution.py:256
  50.5 0.0 copy-start.2
  50.5 1.9 %copy.16 = bf16[128,2048]{1,0:T(8,128)(2,1)} copy(bf16[128,2048]{1,0:T(8,128)(2,1)} %get-tuple-element.8) | data formatting | bytes 1048576
  52.5 0.0 copy-done.2
  52.5 0.0 copy-start.1
  52.5 0.7 %copy.17 = bf16[128,512]{1,0:T(8,128)(2,1)} copy(bf16[128,512]{1,0:T(8,128)(2,1)S(1)} %copy-done.2) | data formatting | bytes 262144
  53.1 0.3 copy-done.1
  53.4 0.0 copy-start
  53.4 0.7 %copy.18 = bf16[128,512]{1,0:T(8,128)(2,1)} copy(bf16[128,512]{1,0:T(8,128)(2,1)S(1)} %copy-done.1) | data formatting | bytes 262144
  54.1 0.3 copy-done
  54.4 0.7 %copy.19 = bf16[128,512]{1,0:T(8,128)(2,1)} copy(bf16[128,512]{1,0:T(8,128)(2,1)S(1)} %copy-done) | data formatting | bytes 262144
Async XLA Ops:
  50.5 1.9 %copy-start.2 = (bf16[128,512]{1,0:T(8,128)(2,1)S(1)}, bf16[128,512]{1,0:T(8,128)(2,1)}, u32[]{:S(2)}) copy-start(bf16[128,512]{1,0:T(8,128)(2,1)} %get-tuple-element.9) | copy-start | bytes 393220
  52.5 1.0 %copy-start.1 = (bf16[128,512]{1,0:T(8,128)(2,1)S(1)}, bf16[128,512]{1,0:T(8,128)(2,1)}, u32[]{:S(2)}) copy-start(bf16[128,512]{1,0:T(8,128)(2,1)} %get-tuple-element.10) | copy-start | bytes 393220
  53.4 1.0 %copy-start = (bf16[128,512]{1,0:T(8,128)(2,1)S(1)}, bf16[128,512]{1,0:T(8,128)(2,1)}, u32[]{:S(2)}) copy-start(bf16[128,512]{1,0:T(8,128)(2,1)} %get-tuple-element.11) | copy-start | bytes 393220
